TPU v7x, 32 devices: a whole 2x2x4 slice. The times are simulated.
32 devices in a mesh: sector: 16 (over z, y, x), op: 2 (over core).
Axes of the slice: x: 2, y: 2, z: 4, core: 2. Of those that a mesh axis runs over, the one named last changes fastest.
Arguments:
- psi: bfloat16 [1024, 128, 128], P('sector'), may hold values from -6 to 6
- left_env: bfloat16 [2, 128, 128, 128], P('op', 'sector'), may hold values from -0.5 to 0.5
- right_env: bfloat16 [2, 128, 128, 128], P('op', 'sector'), may hold values from -0.375 to 0.375
- left_dims: int32 [128], replicated, may hold values from 64 to 128
- right_dims: int32 [128], replicated, may hold values from 64 to 128
- block_right: int32 [1024], replicated, may hold values from 0 to 127, as said below
Outputs:
- h_psi: bfloat16 [1024, 128, 128], P('sector', 'op')
Inputs may be any that keep to these rules, and one draw needn't show every extreme that they name: Block d * 64 + j lies in left sector d * 8 + j // 8; its right sector is owned by index block_right // 8 of sector, and block_right % 8 equals j // 8. Of the 64 blocks of each index of sector, exactly 4 have their right sector owned by each index of sector; the 8 blocks of one left sector have distinct right sectors, and every right sector is paired with exactly 8 blocks.
All inputs are finite; a program needn't handle non-finite values.
Results may differ from a plain program's by a relative error of at most 0.0049.
Values may be sent and summed in bfloat16 or wider, within the bound.
A program may use at most 64 MiB of HBM per device.

v0:
```python
import jax
import jax.numpy as jnp
from jax import lax
from jax.sharding import PartitionSpec as P


def combine(partial_sum):
    row_count = partial_sum.shape[1] // lax.axis_size("op")
    whole = lax.psum(partial_sum, "op")
    return lax.dynamic_slice_in_dim(whole, lax.axis_index("op") * row_count, row_count, 1)


def per_device(psi, left_env, right_env, left_dims, right_dims, block_right):
    devices = lax.axis_size("sector")
    sector_index = lax.axis_index("sector")
    blocks = psi.shape[0]
    block_width = psi.shape[1]
    term_count = left_env.shape[0]
    sectors = left_env.shape[1]
    coupled = blocks // sectors
    slot_count = blocks // devices
    counter = jnp.arange(blocks, dtype=jnp.int32)
    mine_right = lax.dynamic_slice_in_dim(block_right, sector_index * blocks, blocks)
    mine_owner = mine_right // sectors
    send_order = jnp.argsort(mine_owner * blocks + counter)
    inverse = jnp.argsort(send_order)
    own_dims = lax.dynamic_slice_in_dim(left_dims, sector_index * sectors, sectors)
    row_limit = jnp.repeat(own_dims, coupled)
    col_limit = right_dims[mine_right]
    position = jnp.arange(block_width, dtype=jnp.int32)
    keep_mask = (position[None, :, None] < row_limit[:, None, None]) & (
        position[None, None, :] < col_limit[:, None, None]
    )
    masked = psi * keep_mask.astype(psi.dtype)
    products = jnp.einsum(
        "ksab,snbc->ksnac",
        left_env,
        masked.reshape(sectors, coupled, block_width, block_width),
        preferred_element_type=jnp.float32,
    )
    products = products.astype(jnp.bfloat16).reshape(term_count, blocks, block_width, block_width)
    owners_all = (block_right // sectors).reshape(devices, blocks)
    foreign = (owners_all != sector_index).astype(jnp.int32)
    incoming = jnp.argsort(foreign * blocks + counter[None, :], axis=1)[:, :slot_count]
    arriving = (
        jnp.take_along_axis(block_right.reshape(devices, blocks), incoming, axis=1).reshape(-1)
        - sector_index * sectors
    )
    outgoing = right_env[:, arriving].reshape(
        term_count, devices, slot_count, block_width, block_width
    )
    received = lax.all_to_all(outgoing, "sector", split_axis=1, concat_axis=1, tiled=True)
    chosen = received.reshape(term_count, blocks, block_width, block_width)[:, inverse]
    partial_sum = jnp.einsum("kjab,kjcb->jac", products, chosen, preferred_element_type=jnp.float32)
    result = combine(partial_sum).astype(jnp.bfloat16)
    row_count = result.shape[1]
    op_index = lax.axis_index("op")
    row_position = op_index * row_count + jnp.arange(row_count, dtype=jnp.int32)
    keep_rows = (row_position[None, :, None] < row_limit[:, None, None]) & (
        position[None, None, :] < col_limit[:, None, None]
    )
    return result * keep_rows.astype(jnp.bfloat16)


def solution(mesh):
    in_specs = (
        P("sector", None, None),
        P("op", "sector", None, None),
        P("op", "sector", None, None),
        P(),
        P(),
        P(),
    )
    out_specs = P("sector", "op", None)
    return jax.shard_map(
        per_device, mesh=mesh, in_specs=in_specs, out_specs=out_specs, check_vma=False
    )
```

profile of v0, /device:TPU:13, one launch (start us, length us, event | category | flops | bytes accessed | tf_op | source)
XLA Modules:
  0.0 86.6 jit_solution(15736413275250530421)
XLA Ops:
  0.0 0.0 copy-start
  0.0 0.8 reshape.167
  0.8 0.7 fusion.4
  1.5 0.1 mul.34
  1.6 0.1 copy.23
  1.7 1.0 %sort.48 = (s32[16,64]{0,1:T(8,128)}, s32[16,64]{0,1:T(8,128)S(1)}) sort(s32[16,64]{0,1:T(8,128)S(1)} %iota_add_fusion, s32[16,64]{0,1:T(8,128)S(1)} %iota.41), dimensions={1}, to_apply=%region_0.1 | sort | flops 10240 | bytes 16384 | tf_op jit(solution)/shard_map/jit(argsort)/sort | solution.py:44
  2.7 0.1 copy.24
  2.8 0.1 reshape.200
  2.9 0.8 gather_fusion.3
  3.7 0.1 reshape.203
  3.8 0.1 copy.25
  3.9 0.1 copy.26
  4.0 0.1 sub.31
  4.1 2.2 %gather_fusion.1 = bf16[64,128,128]{2,1,0:T(8,128)(2,1)} fusion(bf16[8,128,128]{2,1,0:T(8,128)(2,1)S(1)} %bitcast.24, s32[1024]{0:T(1024)S(1)} %pad_clamp_fusion.1), kind=kCustom, calls=%fused_computation.1 | custom fusion | bytes 4194560 | tf_op jit(solution)/shard_map/gather | solution.py:49
  6.3 6.7 %all-to-all-start = ((bf16[1,16,4,128,128]{4,3,2,0,1:T(8,128)(2,1)}), bf16[1,16,4,128,128]{4,3,2,0,1:T(8,128)(2,1)S(1)}, u32[]{:S(2)}, u32[]{:S(2)}) async-start(bf16[1,16,4,128,128]{4,3,2,0,1:T(8,128)(2,1)} %bitcast.26), calls=%async_computation | async-start | bytes 4194304 | tf_op jit(solution)/shard_map/all_to_all | solution.py:52
  13.0 0.1 dynamic_slice.9
  13.1 0.1 broadcast_in_dim.10
  13.2 0.1 lt.98
  13.2 0.8 iota_add_fusion.1
  14.0 0.8 gather_fusion
  14.8 2.0 %sort.49 = (s32[64]{0:T(128)}, s32[64]{0:T(128)S(1)}) sort(s32[64]{0:T(128)S(1)} %get-tuple-element.11, s32[64]{0:T(128)S(1)} %iota.43), dimensions={0}, to_apply=%region_1.2 | sort | flops 384 | bytes 1024 | tf_op jit(solution)/shard_map/jit(argsort)/sort | solution.py:25
  16.9 2.0 %sort.50 = (s32[64]{0:T(128)}, s32[64]{0:T(128)S(1)}) sort(s32[64]{0:T(128)S(1)} %get-tuple-element.9, s32[64]{0:T(128)S(1)} %iota.44), dimensions={0}, to_apply=%region_2.3 | sort | flops 384 | bytes 1024 | tf_op jit(solution)/shard_map/jit(argsort)/sort | solution.py:26
  18.9 0.1 broadcast_compare_fusion
  19.0 0.1 iota_compare_fusion
  19.1 0.0 copy-start.2
  19.1 3.2 %and_select_fusion = bf16[64,128,128]{2,1,0:T(8,128)(2,1)S(1)} fusion(bf16[64,128,128]{2,1,0:T(8,128)(2,1)} %param.6, pred[64,128]{1,0:T(8,128)(4,1)S(1)} %get-tuple-element.14, pred[64,128]{1,0:T(8,128)(4,1)S(1)} %get-tuple-element.13), kind=kLoop, calls=%fused_computation.4 | loop fusion | flops 2097152 | bytes 4210688 | tf_op jit(solution)/shard_map/mul | solution.py:34
  22.3 2.1 %convolution_convert_fusion = bf16[8,8,128,128]{3,2,1,0:T(8,128)(2,1)} fusion(bf16[8,8,128,128]{3,2,1,0:T(8,128)(2,1)S(1)} %bitcast.27, bf16[1,8,128,128]{3,2,1,0:T(8,128)(2,1)S(1)} %copy-done.2), kind=kOutput, calls=%fused_computation.7 | convolution fusion | flops 269484032 | bytes 4456448 | tf_op jit(solution)/shard_map/ksab,snbc->ksnac/dot_general | solution.py:35
  24.5 36.5 %all-to-all-done = bf16[1,16,4,128,128]{4,3,2,0,1:T(8,128)(2,1)S(1)} async-done(((bf16[1,16,4,128,128]{4,3,2,0,1:T(8,128)(2,1)}), bf16[1,16,4,128,128]{4,3,2,0,1:T(8,128)(2,1)S(1)}, u32[]{:S(2)}, u32[]{:S(2)}) %all-to-all-start) | async-done | bytes 2097184 | tf_op jit(solution)/shard_map/all_to_all | solution.py:52
  61.0 2.2 %gather_fusion.2 = bf16[64,128,128]{2,1,0:T(8,128)(2,1)} fusion(bf16[64,128,128]{2,1,0:T(8,128)(2,1)S(1)} %bitcast.25, s32[1024]{0:T(1024)S(1)} %pad_clamp_fusion), kind=kCustom, calls=%fused_computation.2 | custom fusion | bytes 4194560 | tf_op jit(solution)/shard_map/gather | solution.py:53
  63.1 5.8 %fusion.6 = f32[64,128,128]{2,1,0:T(8,128)} fusion(bf16[64,128,128]{1,2,0:T(8,128)(2,1)} %bitcast.28, bf16[64,128,128]{2,1,0:T(8,128)(2,1)} %gather_fusion.2), kind=kOutput, calls=%fused_computation.38 | convolution fusion | flops 268435456 | bytes 8388608 | tf_op jit(solution)/shard_map/kjab,kjcb->jac/dot_general | solution.py:54
  68.9 16.2 %all-reduce.1 = bf16[64,128,128]{2,1,0:T(8,128)(2,1)S(1)} all-reduce(f32[64,128,128]{2,1,0:T(8,128)} %fusion.6), channel_id=1, replica_groups=mesh['sector'=16,'op'=2] {'op'}, use_global_device_ids=true, to_apply=%region_3.4 | all-reduce | flops 1048576 | bytes 6291456 | tf_op jit(solution)/shard_map/psum | solution.py:9
  85.1 1.5 %and_select_fusion.1 = bf16[64,64,128]{2,1,0:T(8,128)(2,1)} fusion(bf16[64,128,128]{2,1,0:T(8,128)(2,1)S(1)} %all-reduce.1, s32[]{:T(128)S(6)} %select_n.61, pred[64,128]{1,0:T(8,128)(4,1)S(1)} %get-tuple-element.14, pred[64,64]{1,0:T(8,128)(4,1)S(1)} %broadcast_compare_fusion), kind=kLoop, calls=%fused_computation.6 | loop fusion | flops 1048576 | bytes 2109444 | tf_op jit(solution)/shard_map/mul | solution.py:62
  (18 shorter events, 0.1 us)
Async XLA Ops:
  0.0 4.1 %copy-start = (bf16[1,8,128,128]{3,2,1,0:T(8,128)(2,1)S(1)}, bf16[1,8,128,128]{3,2,1,0:T(8,128)(2,1)}, u32[]{:S(2)}) copy-start(bf16[1,8,128,128]{3,2,1,0:T(8,128)(2,1)} %param.8) | copy-start | bytes 786436
  6.3 6.7 %copy-start.3 = (s32[128]{0:T(128)S(1)}, s32[128]{0:T(128)}, u32[]{:S(2)}) copy-start(s32[128]{0:T(128)} %param.9) | copy-start | bytes 1540
  6.3 7.8 %copy-start.1 = (s32[128]{0:T(128)S(1)}, s32[128]{0:T(128)}, u32[]{:S(2)}) copy-start(s32[128]{0:T(128)} %param.10) | copy-start | bytes 1540
  6.3 54.7 %all-to-all-start = ((bf16[1,16,4,128,128]{4,3,2,0,1:T(8,128)(2,1)}), bf16[1,16,4,128,128]{4,3,2,0,1:T(8,128)(2,1)S(1)}, u32[]{:S(2)}, u32[]{:S(2)}) async-start(bf16[1,16,4,128,128]{4,3,2,0,1:T(8,128)(2,1)} %bitcast.26), calls=%async_computation | async-start | bytes 4194304 | tf_op jit(solution)/shard_map/all_to_all | solution.py:52
  19.1 3.2 %copy-start.2 = (bf16[1,8,128,128]{3,2,1,0:T(8,128)(2,1)S(1)}, bf16[1,8,128,128]{3,2,1,0:T(8,128)(2,1)}, u32[]{:S(2)}) copy-start(bf16[1,8,128,128]{3,2,1,0:T(8,128)(2,1)} %param.7) | copy-start | bytes 786436
where the time goes:
time: 86.9 us; the launch traced here: 86.6 us
  waiting for transfers between devices  36.5 us (42%)
  blocking collectives  16.2 us (19%)
  other arithmetic  11.5 us (13%)
  matrix products  7.91 us (9%)
  local copies, waits for them, and re-layouts  7.65 us (9%)
  starting transfers between devices  6.74 us (8%)
    all_to_all x1, waiting for transfers between devices, per_device(): lax.all_to_all(outgoing, 'sector', split_axis=1, concat_axis=1, tiled=True)  36.5 us
    psum x1, blocking collectives, combine(): whole = lax.psum(partial_sum, 'op')  16.2 us
    all_to_all x1, starting transfers between devices, per_device(): lax.all_to_all(outgoing, 'sector', split_axis=1, concat_axis=1, tiled=True)  6.74 us
    dot_general x1, matrix products, per_device(): jnp.einsum('kjab,kjcb->jac', products, chosen, preferred_element_type=jnp...  5.76 us
    mul x1, other arithmetic, per_device(): masked = psi * keep_mask.astype(psi.dtype)  3.23 us
    gather x1, local copies, waits for them, and re-layouts, per_device(): right_env[:, arriving]  2.17 us
    gather x1, local copies, waits for them, and re-layouts, per_device(): received.reshape(term_count, blocks, block_width, block_width)[:, inverse]  2.16 us
    dot_general x1, matrix products, per_device(): jnp.einsum('ksab,snbc->ksnac', left_env, masked.reshape(sectors, coupled,...  2.15 us
  transfers between devices with their start and end apart: 1, of which 1 were waited for; matrix products, arithmetic and copies ran while one was open for 13% of the time, Pallas kernels for 0%

commit v1 on v0

--- a/solution.py
+++ b/solution.py
@@ -49,7 +49,10 @@
     outgoing = right_env[:, arriving].reshape(
         term_count, devices, slot_count, block_width, block_width
     )
-    received = lax.all_to_all(outgoing, "sector", split_axis=1, concat_axis=1, tiled=True)
+    devices_2 = lax.axis_size("sector")
+    pieces = jnp.stack(jnp.split(outgoing, devices_2, axis=1), axis=0)
+    pieces = lax.all_to_all(pieces, "sector", split_axis=0, concat_axis=0)
+    received = jnp.concatenate(pieces, axis=1)
     chosen = received.reshape(term_count, blocks, block_width, block_width)[:, inverse]
     partial_sum = jnp.einsum("kjab,kjcb->jac", products, chosen, preferred_element_type=jnp.float32)
     result = combine(partial_sum).astype(jnp.bfloat16)

time: 86.9 us -> 97 us (1.12)
  local copies, waits for them, and re-layouts: 7.65 us -> 17 us
    unnamed x8 -> x23, local copies, waits for them, and re-layouts: 0.02 us -> 9.88 us
    gather x1, local copies, waits for them, and re-layouts: 2.17 us -> 0.95 us  [per_device(): right_env[:, arriving]]
  transfers between devices with their start and end apart: 1 -> 1, of which waited for: 1 -> 1; matrix products, arithmetic and copies ran while one was open for 13% -> 11% of each run, Pallas kernels for 0% -> 0%
where the time goes in v1:
time: 97 us; the launch traced here: 96.7 us
  waiting for transfers between devices  37.2 us (38%)
  local copies, waits for them, and re-layouts  17 us (18%)
  blocking collectives  16.2 us (17%)
  other arithmetic  11.6 us (12%)
  matrix products  7.91 us (8%)
  starting transfers between devices  6.74 us (7%)
    all_to_all x1, waiting for transfers between devices, per_device(): pieces = lax.all_to_all(pieces, 'sector', split_axis=0, concat_axis=0)  37.2 us
    psum x1, blocking collectives, combine(): whole = lax.psum(partial_sum, 'op')  16.2 us
    unnamed x23, local copies, waits for them, and re-layouts  9.88 us
    all_to_all x1, starting transfers between devices, per_device(): pieces = lax.all_to_all(pieces, 'sector', split_axis=0, concat_axis=0)  6.74 us
    dot_general x1, matrix products, per_device(): jnp.einsum('kjab,kjcb->jac', products, chosen, preferred_element_type=jnp...  5.76 us
    mul x1, other arithmetic, per_device(): masked = psi * keep_mask.astype(psi.dtype)  3.23 us
    gather x1, local copies, waits for them, and re-layouts, per_device(): received.reshape(term_count, blocks, block_width, block_width)[:, inverse]  2.16 us
    dot_general x1, matrix products, per_device(): jnp.einsum('ksab,snbc->ksnac', left_env, masked.reshape(sectors, coupled,...  2.15 us
  transfers between devices with their start and end apart: 1, of which 1 were waited for; matrix products, arithmetic and copies ran while one was open for 11% of the time, Pallas kernels for 0%

profile of v1, /device:TPU:13, one launch (start us, length us, event | category | flops | bytes accessed | tf_op | source)
XLA Modules:
  0.0 96.7 jit_solution(10176076833489912751)
XLA Ops:
  0.0 0.8 reshape.164
  0.8 0.7 fusion.20
  1.5 0.8 iota_add_fusion.1
  2.4 1.0 %sort.48 = (s32[16,64]{0,1:T(8,128)}, s32[16,64]{0,1:T(8,128)S(1)}) sort(s32[16,64]{0,1:T(8,128)S(1)} %iota_add_fusion, s32[16,64]{0,1:T(8,128)S(1)} %iota.41), dimensions={1}, to_apply=%region_0.1 | sort | flops 10240 | bytes 16384 | tf_op jit(solution)/shard_map/jit(argsort)/sort | solution.py:44
  3.7 0.8 gather_fusion.3
  4.9 1.0 gather_fusion.1
  5.8 0.6 fusion.16
  6.5 0.7 fusion.15
  7.1 0.7 fusion.14
  7.8 0.7 fusion.13
  8.5 0.7 fusion.12
  9.8 0.7 fusion.10
  10.4 0.7 fusion.9
  11.1 0.7 fusion.8
  11.8 0.7 fusion.7
  12.4 0.7 fusion.6
  13.1 0.7 fusion.5
  13.7 0.7 fusion.4
  14.4 0.7 fusion.3
  15.0 0.6 fusion.2
  15.7 0.7 fusion.1
  16.4 6.7 %all-to-all-start = ((bf16[16,1,1,4,128,128]{5,4,3,2,1,0:T(8,128)(2,1)}), bf16[16,1,1,4,128,128]{5,4,3,2,1,0:T(8,128)(2,1)S(1)}, u32[]{:S(2)}, u32[]{:S(2)}) async-start(bf16[16,1,1,4,128,128]{5,4,3,2,1,0:T(8,128)(2,1)} %fusion.1), calls=%async_computation | async-start | bytes 4194304 | tf_op jit(solution)/shard_map/all_to_all | solution.py:54
  23.3 2.0 %sort.49 = (s32[64]{0:T(128)}, s32[64]{0:T(128)S(1)}) sort(s32[64]{0:T(128)S(1)} %get-tuple-element.11, s32[64]{0:T(128)S(1)} %iota.43), dimensions={0}, to_apply=%region_1.2 | sort | flops 384 | bytes 1024 | tf_op jit(solution)/shard_map/jit(argsort)/sort | solution.py:25
  25.4 2.0 %sort.50 = (s32[64]{0:T(128)}, s32[64]{0:T(128)S(1)}) sort(s32[64]{0:T(128)S(1)} %get-tuple-element.9, s32[64]{0:T(128)S(1)} %iota.44), dimensions={0}, to_apply=%region_2.3 | sort | flops 384 | bytes 1024 | tf_op jit(solution)/shard_map/jit(argsort)/sort | solution.py:26
  27.4 0.8 gather_fusion
  28.5 3.2 %and_select_fusion = bf16[64,128,128]{2,1,0:T(8,128)(2,1)S(1)} fusion(bf16[64,128,128]{2,1,0:T(8,128)(2,1)} %param.6, pred[64,128]{1,0:T(8,128)(4,1)S(1)} %iota_compare_fusion.1, pred[64,128]{1,0:T(8,128)(4,1)S(1)} %iota_compare_fusion), kind=kLoop, calls=%fused_computation.4 | loop fusion | flops 2097152 | bytes 4210688 | tf_op jit(solution)/shard_map/mul | solution.py:34
  31.7 2.1 %convolution_convert_fusion = bf16[8,8,128,128]{3,2,1,0:T(8,128)(2,1)} fusion(bf16[8,8,128,128]{3,2,1,0:T(8,128)(2,1)S(1)} %bitcast.106, bf16[1,8,128,128]{3,2,1,0:T(8,128)(2,1)S(1)} %copy-done.2), kind=kOutput, calls=%fused_computation.7 | convolution fusion | flops 269484032 | bytes 4456448 | tf_op jit(solution)/shard_map/ksab,snbc->ksnac/dot_general | solution.py:35
  33.9 37.2 %all-to-all-done = bf16[16,1,1,4,128,128]{5,4,3,2,1,0:T(8,128)(2,1)S(1)} async-done(((bf16[16,1,1,4,128,128]{5,4,3,2,1,0:T(8,128)(2,1)}), bf16[16,1,1,4,128,128]{5,4,3,2,1,0:T(8,128)(2,1)S(1)}, u32[]{:S(2)}, u32[]{:S(2)}) %all-to-all-start) | async-done | bytes 2097184 | tf_op jit(solution)/shard_map/all_to_all | solution.py:54
  71.1 2.2 %gather_fusion.2 = bf16[64,128,128]{2,1,0:T(8,128)(2,1)} fusion(bf16[64,128,128]{2,1,0:T(8,128)(2,1)S(1)} %bitcast.105, s32[1024]{0:T(1024)S(1)} %pad_clamp_fusion), kind=kCustom, calls=%fused_computation.2 | custom fusion | bytes 4194560 | tf_op jit(solution)/shard_map/gather | solution.py:56
  73.2 5.8 %fusion.22 = f32[64,128,128]{2,1,0:T(8,128)} fusion(bf16[64,128,128]{1,2,0:T(8,128)(2,1)} %bitcast.107, bf16[64,128,128]{2,1,0:T(8,128)(2,1)} %gather_fusion.2), kind=kOutput, calls=%fused_computation.70 | convolution fusion | flops 268435456 | bytes 8388608 | tf_op jit(solution)/shard_map/kjab,kjcb->jac/dot_general | solution.py:57
  79.0 16.2 %all-reduce.1 = bf16[64,128,128]{2,1,0:T(8,128)(2,1)S(1)} all-reduce(f32[64,128,128]{2,1,0:T(8,128)} %fusion.22), channel_id=1, replica_groups=mesh['sector'=16,'op'=2] {'op'}, use_global_device_ids=true, to_apply=%region_3.4 | all-reduce | flops 1048576 | bytes 6291456 | tf_op jit(solution)/shard_map/psum | solution.py:9
  95.2 1.5 %and_select_fusion.1 = bf16[64,64,128]{2,1,0:T(8,128)(2,1)} fusion(bf16[64,128,128]{2,1,0:T(8,128)(2,1)S(1)} %all-reduce.1, s32[]{:T(128)S(6)} %select_n.61, pred[64,128]{1,0:T(8,128)(4,1)S(1)} %iota_compare_fusion.1, pred[64,64]{1,0:T(8,128)(4,1)S(1)} %broadcast_compare_fusion), kind=kLoop, calls=%fused_computation.6 | loop fusion | flops 1048576 | bytes 2109444 | tf_op jit(solution)/shard_map/mul | solution.py:65
  (34 shorter events, 1.9 us)
Async XLA Ops:
  0.0 4.9 %copy-start = (bf16[1,8,128,128]{3,2,1,0:T(8,128)(2,1)S(1)}, bf16[1,8,128,128]{3,2,1,0:T(8,128)(2,1)}, u32[]{:S(2)}) copy-start(bf16[1,8,128,128]{3,2,1,0:T(8,128)(2,1)} %param.8) | copy-start | bytes 786436
  16.4 6.7 %copy-start.3 = (s32[128]{0:T(128)S(1)}, s32[128]{0:T(128)}, u32[]{:S(2)}) copy-start(s32[128]{0:T(128)} %param.9) | copy-start | bytes 1540
  16.4 11.1 %copy-start.1 = (s32[128]{0:T(128)S(1)}, s32[128]{0:T(128)}, u32[]{:S(2)}) copy-start(s32[128]{0:T(128)} %param.10) | copy-start | bytes 1540
  16.4 54.7 %all-to-all-start = ((bf16[16,1,1,4,128,128]{5,4,3,2,1,0:T(8,128)(2,1)}), bf16[16,1,1,4,128,128]{5,4,3,2,1,0:T(8,128)(2,1)S(1)}, u32[]{:S(2)}, u32[]{:S(2)}) async-start(bf16[16,1,1,4,128,128]{5,4,3,2,1,0:T(8,128)(2,1)} %fusion.1), calls=%async_computation | async-start | bytes 4194304 | tf_op jit(solution)/shard_map/all_to_all | solution.py:54
  28.5 3.2 %copy-start.2 = (bf16[1,8,128,128]{3,2,1,0:T(8,128)(2,1)S(1)}, bf16[1,8,128,128]{3,2,1,0:T(8,128)(2,1)}, u32[]{:S(2)}) copy-start(bf16[1,8,128,128]{3,2,1,0:T(8,128)(2,1)} %param.7) | copy-start | bytes 786436
